TPU v7x, 32 devices: a whole 2x2x4 slice. The times are simulated.
32 devices in a mesh: seq: 8 (over y, x, core), mp: 4 (over z).
Axes of the slice: x: 2, y: 2, z: 4, core: 2. Of those that a mesh axis runs over, the one named last changes fastest.
Arguments:
- stream: float32 [4096, 2048], P('seq', 'mp'), may hold values from -6 to 6
- doc_starts: int32 [4096], P('seq'), may hold values 0 or 1
- gain_first: float32 [2048], replicated, may hold values from 0.5 to 1.5
- proj_inner: bfloat16 [2048, 2560], P(None, 'mp'), may hold values from -0.125 to 0.125
- proj_gate: bfloat16 [2048, 2560], P(None, 'mp'), may hold values from -0.125 to 0.125
- conv_weight: float32 [4, 2560], P(None, 'mp'), may hold values from -3 to 3
- conv_bias: float32 [2560], P('mp'), may hold values from -3 to 3
- gate_recur: bfloat16 [16, 160, 160], P('mp'), may hold values from -0.5 to 0.5
- gate_input: bfloat16 [16, 160, 160], P('mp'), may hold values from -0.5 to 0.5
- bias_recur: float32 [2560], P('mp'), may hold values from -3 to 3
- bias_input: float32 [2560], P('mp'), may hold values from -3 to 3
- decay_param: float32 [2560], P('mp'), may hold values from 3.4 to 15, as said below
- proj_out: bfloat16 [2560, 2048], P('mp'), may hold values from -0.25 to 0.25
- gain_second: float32 [2048], replicated, may hold values from 0.5 to 1.5
- mlp_gate: bfloat16 [2048, 6144], P(None, 'mp'), may hold values from -0.125 to 0.125
- mlp_up: bfloat16 [2048, 6144], P(None, 'mp'), may hold values from -0.125 to 0.125
- mlp_down: bfloat16 [6144, 2048], P('mp'), may hold values from -0.15625 to 0.15625
- cotangent: float32 [4096, 2048], P('seq', 'mp'), may hold values from -6 to 6
Outputs:
- output: float32 [4096, 2048], P('seq', 'mp')
- grad_stream: float32 [4096, 2048], P('seq', 'mp')
- grad_gain_first: float32 [2048], replicated
- grad_proj_inner: float32 [2048, 2560], P('seq', 'mp')
- grad_proj_gate: float32 [2048, 2560], P('seq', 'mp')
- grad_conv_weight: float32 [4, 2560], P(None, 'mp')
- grad_conv_bias: float32 [2560], P('mp')
- grad_gate_recur: float32 [16, 160, 160], P('mp')
- grad_gate_input: float32 [16, 160, 160], P('mp')
- grad_bias_recur: float32 [2560], P('mp')
- grad_bias_input: float32 [2560], P('mp')
- grad_decay: float32 [2560], P('mp')
- grad_proj_out: float32 [2560, 2048], P(('mp', 'seq'))
- grad_gain_second: float32 [2048], replicated
- grad_mlp_gate: float32 [2048, 6144], P('seq', 'mp')
- grad_mlp_up: float32 [2048, 6144], P('seq', 'mp')
- grad_mlp_down: float32 [6144, 2048], P(('mp', 'seq'))
Inputs may be any that keep to these rules, and one draw needn't show every extreme that they name: decay_param is -log(exp(q) - 1) for a per-channel rate q between 0.05 / 4096 and 0.03. `doc_starts`: a 1 marks the first token of a document.
All inputs are finite; a program needn't handle non-finite values. No bound on the sum of `doc_starts` on one device may be relied on, other than what follows from the above.
Results may differ from a plain program's by a relative error of at most 0.0089.
Values sent between devices are 32-bit elements; how exact they have to be, the bound alone decides.
No kernel may reach another device: no remote copies, remote signals or barrier semaphores. Data moves between devices by JAX's collectives and lax.ppermute only.
A program may use at most 256 MiB of HBM per device.

v0:
```python
from functools import partial
import jax
import jax.numpy as jnp
from jax import lax
from jax.sharding import PartitionSpec as P

recur_scale = 8.0
norm_eps = 1e-06


def passed_along(value, axis, steps):
    count = lax.axis_size(axis)
    first, last = (max(0, -steps), min(count, count - steps))
    return lax.ppermute(value, axis, [(source, source + steps) for source in range(first, last)])


def carried_in(value, axis, join, neutral, backward):
    count, mine = (lax.axis_size(axis), lax.axis_index(axis))
    pieces = jax.tree.map(lambda part: lax.all_gather(part, axis), value)
    if backward:
        pieces = jax.tree.map(lambda part: part[::-1], pieces)
        mine = count - 1 - mine
    running = jax.tree.map(
        lambda part, zero: jnp.full_like(part, 0) + jnp.asarray(zero, part.dtype), value, neutral
    )

    def turn(position, running):
        longer = join(running, jax.tree.map(lambda part: part[position], pieces))
        return jax.tree.map(lambda new, old: jnp.where(position < mine, new, old), longer, running)

    return lax.fori_loop(0, count - 1, turn, running)


def norm_rows(rows, gain):
    return rows * lax.rsqrt(jnp.mean(rows * rows, axis=-1, keepdims=True) + norm_eps) * gain


def matmul(left, right):
    return jnp.dot(left, right, preferred_element_type=jnp.float32)


def matmul_nt(left, right):
    return lax.dot_general(
        left, right, (((1,), (1,)), ((), ())), preferred_element_type=jnp.float32
    )


def matmul_tn(left, right):
    return lax.dot_general(
        left, right, (((0,), (0,)), ((), ())), preferred_element_type=jnp.float32
    )


def block_apply(values, weights):
    count = values.shape[0]
    groups = weights.shape[0]
    width = weights.shape[1]
    split = values.reshape(count, groups, width)
    mixed = jnp.einsum("tbi,bio->tbo", split, weights, preferred_element_type=jnp.float32)
    return mixed.reshape(count, groups * width)


def block_back(grads, weights):
    count = grads.shape[0]
    groups = weights.shape[0]
    width = weights.shape[1]
    split = grads.reshape(count, groups, width)
    mixed = jnp.einsum("tbo,bio->tbi", split, weights, preferred_element_type=jnp.float32)
    return mixed.reshape(count, groups * width)


def block_grad(values, grads, groups):
    count = values.shape[0]
    width = values.shape[1] // groups
    left = values.reshape(count, groups, width)
    right = grads.reshape(count, groups, width)
    return jnp.einsum("tbi,tbo->bio", left, right, preferred_element_type=jnp.float32)


def link(earlier, later):
    return (later[0] * earlier[0], later[0] * earlier[1] + later[1])


def local_scan(starts, conv_out, recur_pre, input_pre, decay):
    recur = jax.nn.sigmoid(recur_pre)
    entry = jax.nn.sigmoid(input_pre)
    log_decay = -recur_scale * recur * jax.nn.softplus(-decay)
    factor = starts + (1.0 - starts) * jnp.sqrt(-jnp.expm1(2.0 * log_decay))
    carry = jnp.exp(log_decay) * (1.0 - starts)
    fresh = factor * entry * conv_out
    return lax.associative_scan(link, (carry, fresh), axis=0)


def body(
    stream,
    doc_starts,
    gain_first,
    proj_inner,
    proj_gate,
    conv_weight,
    conv_bias,
    gate_recur,
    gate_input,
    bias_recur,
    bias_input,
    decay_param,
    proj_out,
    gain_second,
    mlp_gate,
    mlp_up,
    mlp_down,
    cotangent,
):
    count = stream.shape[0]
    own_width = stream.shape[1]
    inner_width = proj_inner.shape[1]
    ffn_width = mlp_gate.shape[1]
    groups = gate_recur.shape[0]
    lag = conv_weight.shape[0] - 1
    column = lax.axis_index("mp") * own_width
    rows_full = lax.all_gather(stream, "mp", axis=1, tiled=True)
    first_norm, first_back = jax.vjp(norm_rows, rows_full, gain_first)
    first_low = first_norm.astype(jnp.bfloat16)
    inner = matmul(first_low, proj_inner)
    gate_pre = matmul(first_low, proj_gate)
    starts = doc_starts.astype(jnp.float32)[:, None]
    keep = 1.0 - starts
    tail_keep = jnp.concatenate([keep[count - lag + 1 :], jnp.ones((1, 1), jnp.float32)], 0)
    tail_mask = jnp.flip(jnp.cumprod(jnp.flip(tail_keep, 0), 0), 0)
    prior = passed_along(inner[count - lag :] * tail_mask, "seq", 1)
    ext_inner = jnp.concatenate([prior, inner], 0)
    ext_keep = jnp.concatenate([jnp.ones((lag, 1), jnp.float32), keep], 0)
    valid = jnp.ones((count, 1), jnp.float32)
    valids = []
    conv_out = conv_weight[0] * inner
    for k in range(1, lag + 1):
        valid = valid * ext_keep[lag - k + 1 : lag - k + 1 + count]
        valids.append(valid)
        conv_out = conv_out + conv_weight[k] * ext_inner[lag - k : lag - k + count] * valid
    conv_out = conv_out + conv_bias
    conv_low = conv_out.astype(jnp.bfloat16)
    recur_pre = block_apply(conv_low, gate_recur) + bias_recur
    input_pre = block_apply(conv_low, gate_input) + bias_input
    scan_fn = partial(local_scan, starts)
    (span, partial_state), scan_back = jax.vjp(scan_fn, conv_out, recur_pre, input_pre, decay_param)
    identity = (jnp.ones((inner_width,), jnp.float32), jnp.zeros((inner_width,), jnp.float32))
    entering = carried_in(
        (span[count - 1], partial_state[count - 1]), "seq", link, identity, False
    )[1]
    states = span * entering + partial_state
    gated, gelu_back = jax.vjp(jax.nn.gelu, gate_pre)
    mixed_low = (gated * states).astype(jnp.bfloat16)
    branch = lax.psum(matmul(mixed_low, proj_out), "mp")
    resid = rows_full + branch
    second_norm, second_back = jax.vjp(norm_rows, resid, gain_second)
    second_low = second_norm.astype(jnp.bfloat16)
    ffn_gate = matmul(second_low, mlp_gate)
    ffn_up = matmul(second_low, mlp_up)
    ffn_act, act_back = jax.vjp(jax.nn.gelu, ffn_gate)
    hidden_low = (ffn_act * ffn_up).astype(jnp.bfloat16)
    mlp_own = lax.psum_scatter(matmul(hidden_low, mlp_down), "mp", scatter_dimension=1, tiled=True)
    output = lax.dynamic_slice_in_dim(resid, column, own_width, 1) + mlp_own
    cot_full = lax.all_gather(cotangent, "mp", axis=1, tiled=True)
    cot_low = cot_full.astype(jnp.bfloat16)
    d_hidden = matmul_nt(cot_low, mlp_down)
    d_gate_ffn = act_back(d_hidden * ffn_up)[0]
    d_pair_low = jnp.concatenate([d_gate_ffn, d_hidden * ffn_act], 1).astype(jnp.bfloat16)
    d_second_part = matmul_nt(d_pair_low[:, :ffn_width], mlp_gate) + matmul_nt(
        d_pair_low[:, ffn_width:], mlp_up
    )
    d_second = lax.psum(d_second_part, "mp")
    d_resid_norm, d_gain_second = second_back(d_second)
    d_resid = cot_full + d_resid_norm
    branch_low = d_resid.astype(jnp.bfloat16)
    d_mixed = matmul_nt(branch_low, proj_out)
    d_states = d_mixed * gated
    d_gate_low = gelu_back(d_mixed * states)[0].astype(jnp.bfloat16)
    outgoing = jnp.sum(d_states * span, axis=0)
    incoming = carried_in((span[count - 1], outgoing), "seq", link, identity, True)[1]
    d_total = d_states.at[count - 1].add(incoming)
    d_conv_direct, d_recur, d_input, d_decay = scan_back((d_total * entering, d_total))
    d_recur_low = d_recur.astype(jnp.bfloat16)
    d_input_low = d_input.astype(jnp.bfloat16)
    d_conv = (
        d_conv_direct + block_back(d_recur_low, gate_recur) + block_back(d_input_low, gate_input)
    )
    grad_gate_recur = block_grad(conv_low, d_recur_low, groups)
    grad_gate_input = block_grad(conv_low, d_input_low, groups)
    grad_bias_recur = jnp.sum(d_recur_low.astype(jnp.float32), axis=0)
    grad_bias_input = jnp.sum(d_input_low.astype(jnp.float32), axis=0)
    ext_grad = (
        jnp.zeros((count + lag, inner_width), jnp.float32).at[lag:].add(conv_weight[0] * d_conv)
    )
    conv_terms = [jnp.sum(d_conv * inner, axis=0)]
    for k in range(1, lag + 1):
        weighted = d_conv * valids[k - 1]
        ext_grad = ext_grad.at[lag - k : lag - k + count].add(conv_weight[k] * weighted)
        conv_terms.append(jnp.sum(weighted * ext_inner[lag - k : lag - k + count], axis=0))
    grad_conv_weight = jnp.stack(conv_terms, 0)
    grad_conv_bias = jnp.sum(d_conv, axis=0)
    returned = passed_along(ext_grad[:lag], "seq", -1)
    d_inner = ext_grad[lag:].at[count - lag :].add(returned * tail_mask)
    d_inner_low = d_inner.astype(jnp.bfloat16)
    first_pair_low = jnp.concatenate([d_inner_low, d_gate_low], 1)
    d_first_part = matmul_nt(d_inner_low, proj_inner) + matmul_nt(d_gate_low, proj_gate)
    d_first = lax.psum(d_first_part, "mp")
    d_rows_norm, d_gain_first = first_back(d_first)
    grad_stream = lax.dynamic_slice_in_dim(d_resid + d_rows_norm, column, own_width, 1)
    small = lax.psum(
        (
            d_gain_first,
            d_gain_second,
            grad_conv_weight,
            grad_conv_bias,
            grad_gate_recur,
            grad_gate_input,
            grad_bias_recur,
            grad_bias_input,
            d_decay,
        ),
        "seq",
    )
    grad_first, grad_out, grad_pair, grad_down = (
        lax.psum_scatter(
            matmul_tn(first_low, first_pair_low), "seq", scatter_dimension=0, tiled=True
        ),
        lax.psum_scatter(matmul_tn(mixed_low, branch_low), "seq", scatter_dimension=0, tiled=True),
        lax.psum_scatter(matmul_tn(second_low, d_pair_low), "seq", scatter_dimension=0, tiled=True),
        lax.psum_scatter(matmul_tn(hidden_low, cot_low), "seq", scatter_dimension=0, tiled=True),
    )
    return (
        output,
        grad_stream,
        small[0],
        grad_first[:, :inner_width],
        grad_first[:, inner_width:],
        small[2],
        small[3],
        small[4],
        small[5],
        small[6],
        small[7],
        small[8],
        grad_out,
        small[1],
        grad_pair[:, :ffn_width],
        grad_pair[:, ffn_width:],
        grad_down,
    )


def solution(mesh):
    in_specs = (
        P("seq", "mp"),
        P("seq"),
        P(),
        P(None, "mp"),
        P(None, "mp"),
        P(None, "mp"),
        P("mp"),
        P("mp", None, None),
        P("mp", None, None),
        P("mp"),
        P("mp"),
        P("mp"),
        P("mp", None),
        P(),
        P(None, "mp"),
        P(None, "mp"),
        P("mp", None),
        P("seq", "mp"),
    )
    out_specs = (
        P("seq", "mp"),
        P("seq", "mp"),
        P(),
        P("seq", "mp"),
        P("seq", "mp"),
        P(None, "mp"),
        P("mp"),
        P("mp", None, None),
        P("mp", None, None),
        P("mp"),
        P("mp"),
        P("mp"),
        P(("mp", "seq"), None),
        P(),
        P("seq", "mp"),
        P("seq", "mp"),
        P(("mp", "seq"), None),
    )
    return jax.shard_map(body, mesh=mesh, in_specs=in_specs, out_specs=out_specs, check_vma=False)
```

profile of v0, /device:TPU:0, one launch (start us, length us, event | category | flops | bytes accessed | tf_op | source)
XLA Modules:
  0.0 1586.7 jit_solution(3280703168751612168)
XLA Ops:
  10.0 83.1 %all-gather.7.cloned.1.call-done = f32[512,2048]{1,0:T(8,128)} async-done(((f32[512,512]{1,0:T(8,128)}), f32[512,2048]{1,0:T(8,128)}) %all-gather.7.cloned.1.call-update) | async-done | bytes 4194320 | tf_op jit(solution)/shard_map/all_gather | solution.py:121
  103.9 5.4 fusion.68
  240.2 12.3 all-gather.2
  260.7 8.2 all-gather.1
  269.5 5.7 while.34
  275.2 7.2 multiply_convert_fusion.4
  287.9 152.0 %all-reduce.129.cloned.1.call-done = f32[512,2048]{1,0:T(8,128)} async-done(((f32[512,2048]{1,0:T(8,128)}), f32[512,2048]{1,0:T(8,128)}) %all-reduce.129.cloned.1.call-update) | async-done | bytes 4194320 | tf_op jit(solution)/shard_map/psum | solution.py:153
  446.0 10.0 fusion.115
  461.1 60.2 %all-gather.9.cloned.1.call-done = f32[512,2048]{1,0:T(8,128)} async-done(((f32[512,512]{1,0:T(8,128)}), f32[512,2048]{1,0:T(8,128)}) %all-gather.9.cloned.1.call-update) | async-done | bytes 4194320 | tf_op jit(solution)/shard_map/all_gather | solution.py:163
  521.3 12.5 multiply_convert_fusion.2
  533.8 6.7 fusion.117
  540.6 7.9 convolution_add_fusion.1
  551.2 9.5 fusion.116
  560.8 141.4 %all-reduce.131.cloned.1.call-done = f32[512,2048]{1,0:T(8,128)} async-done(((f32[512,2048]{1,0:T(8,128)}), f32[512,2048]{1,0:T(8,128)}) %all-reduce.131.cloned.1.call-update) | async-done | bytes 4194320 | tf_op jit(solution)/shard_map/psum | solution.py:171
  712.3 7.2 multiply_reduce_fusion.11
  719.5 9.0 all-gather.3
  732.1 5.7 while.35
  899.8 5.8 multiply_reduce_fusion.6
  922.2 6.3 multiply_reduce_fusion.9
  952.4 6.8 convolution_add_fusion
  959.3 8.6 fusion.25
  968.0 14.3 fusion.8
  988.0 6.0 fusion.30
  994.1 10.6 fusion.34
  1007.6 106.2 %all-reduce.133.cloned.1.call-done = f32[512,2048]{1,0:T(8,128)} async-done(((f32[512,2048]{1,0:T(8,128)}), f32[512,2048]{1,0:T(8,128)}) %all-reduce.133.cloned.1.call-update) | async-done | bytes 4194320 | tf_op jit(solution)/shard_map/psum | solution.py:206
  1113.8 6.4 multiply_reduce_fusion.1
  1120.2 25.1 %all-reduce.122 = (f32[2048]{0:T(1024)}, f32[4,640]{1,0:T(4,128)}, f32[640]{0:T(1024)}, f32[640]{0:T(1024)}, f32[640]{0:T(1024)}, /*index=5*/f32[640]{0:T(1024)}, f32[2048]{0:T(1024)}) all-reduce(f32[2048]{0:T(1024)S(1)} %get-tuple-element.317, f32[4,640]{1,0:T(4,128)S(1)} %pad_maximum_fusion.15, ...), channel_id=1, replica_groups=mesh['seq'=8,'mp'=4] {'seq'}, use_global_device_ids=true, to_apply=%region_15.16 | all-reduce | flops 9216 | bytes 73728 | tf_op jit(solution)/shard_map/psum | solution.py:209
  1148.4 49.5 %reduce-scatter.8.cloned.1.call-done = f32[256,1280]{1,0:T(8,128)} async-done(((f32[2048,1280]{1,0:T(8,128)}), f32[256,1280]{1,0:T(8,128)}) %reduce-scatter.8.cloned.1.call-update) | async-done | bytes 1310736 | tf_op jit(solution)/shard_map/reduce_scatter | solution.py:224
  1200.3 158.1 %reduce-scatter.12.cloned.1.call-done = f32[256,3072]{1,0:T(8,128)} async-done(((f32[2048,3072]{1,0:T(8,128)}), f32[256,3072]{1,0:T(8,128)}) %reduce-scatter.12.cloned.1.call-update) | async-done | bytes 3145744 | tf_op jit(solution)/shard_map/reduce_scatter | solution.py:228
  1362.1 58.5 %all-reduce.135.cloned.1.call-done = (f32[4,160,160]{2,1,0:T(8,128)}, f32[4,160,160]{2,1,0:T(8,128)}) async-done(((f32[4,160,160]{2,1,0:T(8,128)}, f32[4,160,160]{2,1,0:T(8,128)}), (f32[4,160,160]{2,1,0:T(8,128)}, f32[4,160,160]{2,1,0:T(8,128)})) %all-reduce.135.cloned.1.call-update) | async-done | bytes 819216 | tf_op jit(solution)/shard_map/psum | solution.py:209
  1420.6 60.0 %reduce-scatter.10.cloned.1.call-done = f32[80,2048]{1,0:T(8,128)} async-done(((f32[640,2048]{1,0:T(8,128)}), f32[80,2048]{1,0:T(8,128)}) %reduce-scatter.10.cloned.1.call-update) | async-done | bytes 655376 | tf_op jit(solution)/shard_map/reduce_scatter | solution.py:227
  1480.6 96.5 %reduce-scatter.14.cloned.1.call-done = f32[192,2048]{1,0:T(8,128)} async-done(((f32[1536,2048]{1,0:T(8,128)}), f32[192,2048]{1,0:T(8,128)}) %reduce-scatter.14.cloned.1.call-update) | async-done | bytes 1572880 | tf_op jit(solution)/shard_map/reduce_scatter | solution.py:229
  (810 shorter events, 418.2 us)
Async XLA Ops:
  7.2 268.0 %copy-start = (bf16[2048,640]{1,0:T(8,128)(2,1)S(1)}, bf16[2048,640]{1,0:T(8,128)(2,1)}, u32[]{:S(2)}) copy-start(bf16[2048,640]{1,0:T(8,128)(2,1)} %param.38) | copy-start | bytes 7864324
  7.2 85.9 %all-gather.7.cloned.1.call-start = ((), (), s32[]{:S(2)}) async-start(), calls=%async_computation.5 | async-start | bytes 5242880 | tf_op jit(solution)/shard_map/all_gather | solution.py:121
  7.9 431.9 %all-reduce.129.cloned.1.call-start = ((), (), s32[]{:S(2)}) async-start(), calls=%async_computation.6 | async-start | bytes 8388608 | tf_op jit(solution)/shard_map/psum | solution.py:153
  8.7 112.7 %copy-start.115 = (f32[512]{0:T(512)}, f32[512]{0:T(512)S(1)}, u32[]{:S(2)}) copy-start(f32[512]{0:T(512)S(1)} %broadcast_subtract_fusion) | copy-start | bytes 6148
  9.2 90.9 %copy-start.180 = (f32[3,1]{0,1:T(1,128)}, f32[3,1]{0,1:T(1,128)S(1)}, u32[]{:S(2)}) copy-start(f32[3,1]{0,1:T(1,128)S(1)} %rev.14) | copy-start | bytes 40
  9.3 94.6 %copy-start.160 = (f32[512,1]{0,1:T(1,128)}, f32[512,1]{0,1:T(1,128)S(1)}, u32[]{:S(2)}) copy-start(f32[512,1]{0,1:T(1,128)S(1)} %get-tuple-element.399) | copy-start | bytes 6148
  9.3 94.6 %copy-start.162 = (f32[512,1]{0,1:T(1,128)}, f32[512,1]{0,1:T(1,128)S(1)}, u32[]{:S(2)}) copy-start(f32[512,1]{0,1:T(1,128)S(1)} %get-tuple-element.400) | copy-start | bytes 6148
  9.3 86.5 %copy-start.164 = (f32[2048]{0:T(1024)S(1)}, f32[2048]{0:T(1024)}, u32[]{:S(2)}) copy-start(f32[2048]{0:T(1024)} %param.36) | copy-start | bytes 24580
  10.0 111.4 %copy-start.117 = (f32[640]{0:T(1024)}, f32[640]{0:T(1024)S(1)}, u32[]{:S(2)}) copy-start(f32[640]{0:T(1024)S(1)} %broadcast_multiply_fusion.3) | copy-start | bytes 7684
  101.3 2.6 collective-permute-start
  103.6 17.7 %copy-start.166 = (f32[512]{0:T(512)}, f32[512]{0:T(512)S(1)}, u32[]{:S(2)}) copy-start(f32[512]{0:T(512)S(1)} %convert_element_type.44) | copy-start | bytes 6148
  130.3 22.3 %copy-start.17 = (f32[256,640]{1,0:T(8,128)}, f32[256,640]{1,0:T(8,128)S(1)}, u32[]{:S(2)}) copy-start(f32[256,640]{1,0:T(8,128)S(1)} %slice.594) | copy-start | bytes 1966084
  287.1 234.3 %all-gather.9.cloned.1.call-start = ((), (), s32[]{:S(2)}) async-start(), calls=%async_computation.8 | async-start | bytes 5242880 | tf_op jit(solution)/shard_map/all_gather | solution.py:163
  287.8 156.1 %copy-start.129 = (f32[2048]{0:T(1024)S(1)}, f32[2048]{0:T(1024)}, u32[]{:S(2)}) copy-start(f32[2048]{0:T(1024)} %param.47) | copy-start | bytes 24580
  287.8 414.3 %all-reduce.131.cloned.1.call-start = ((), (), s32[]{:S(2)}) async-start(), calls=%async_computation.9 | async-start | bytes 8388608 | tf_op jit(solution)/shard_map/psum | solution.py:171
  548.5 456.3 %reduce-scatter.6.cloned.1.call-start = ((), (), s32[]{:S(2)}) async-start(), calls=%async_computation.7 | async-start | bytes 5242880 | tf_op jit(solution)/shard_map/reduce_scatter | solution.py:161
  560.7 141.5 %copy-start.170 = (f32[512]{0:T(512)S(1)}, f32[512]{0:T(512)}, u32[]{:S(2)}) copy-start(f32[512]{0:T(512)} %copy-done.169) | copy-start | bytes 6148
  560.7 553.0 %all-reduce.133.cloned.1.call-start = ((), (), s32[]{:S(2)}) async-start(), calls=%async_computation.10 | async-start | bytes 8388608 | tf_op jit(solution)/shard_map/psum | solution.py:206
  803.3 14.4 copy-start.36
  831.0 12.4 slice-start.6
  831.0 12.4 slice-start.7
  946.4 5.3 collective-permute-start.1
  959.3 238.6 %reduce-scatter.8.cloned.1.call-start = ((), (), s32[]{:S(2)}) async-start(), calls=%async_computation.11 | async-start | bytes 11796480 | tf_op jit(solution)/shard_map/reduce_scatter | solution.py:224
  967.9 390.5 %reduce-scatter.12.cloned.1.call-start = ((), (), s32[]{:S(2)}) async-start(), calls=%async_computation.13 | async-start | bytes 28311552 | tf_op jit(solution)/shard_map/reduce_scatter | solution.py:228
  982.3 438.3 %all-reduce.135.cloned.1.call-start = ((), (), s32[]{:S(2)}) async-start(), calls=%async_computation.15 | async-start | bytes 2621440 | tf_op jit(solution)/shard_map/psum | solution.py:209
  986.9 493.7 %reduce-scatter.10.cloned.1.call-start = ((), (), s32[]{:S(2)}) async-start(), calls=%async_computation.12 | async-start | bytes 5898240 | tf_op jit(solution)/shard_map/reduce_scatter | solution.py:227
  994.1 583.0 %reduce-scatter.14.cloned.1.call-start = ((), (), s32[]{:S(2)}) async-start(), calls=%async_computation.14 | async-start | bytes 14155776 | tf_op jit(solution)/shard_map/reduce_scatter | solution.py:229
  1004.8 108.9 %copy-start.159 = (f32[512]{0:T(512)S(1)}, f32[512]{0:T(512)}, u32[]{:S(2)}) copy-start(f32[512]{0:T(512)} %copy-done.158) | copy-start | bytes 6148
  1004.8 108.9 %copy-start.165 = (f32[2048]{0:T(1024)S(1)}, f32[2048]{0:T(1024)}, u32[]{:S(2)}) copy-start(f32[2048]{0:T(1024)} %param.36) | copy-start | bytes 24580
  1007.6 112.6 %copy-start.168 = (f32[2048]{0:T(1024)S(1)}, f32[2048]{0:T(1024)}, u32[]{:S(2)}) copy-start(f32[2048]{0:T(1024)} %get-tuple-element.315) | copy-start | bytes 24580
  1007.6 137.7 %copy-start.173 = (f32[512]{0:T(512)S(1)}, f32[512]{0:T(512)}, u32[]{:S(2)}) copy-start(f32[512]{0:T(512)} %copy-done.172) | copy-start | bytes 6148
  1420.6 158.5 %copy-start.72 = (f32[4,160,160]{2,1,0:T(8,128)S(1)}, f32[4,160,160]{2,1,0:T(8,128)}, u32[]{:S(2)}) copy-start(f32[4,160,160]{2,1,0:T(8,128)} %get-tuple-element.666) | copy-start | bytes 1228804
  (183 other events, 834.8 us)
Sparse Core Ops, SparseCore 0:
  9.6 83.4 all-gather.6
  287.2 152.6 all-reduce.128
  441.5 79.7 all-gather.8
  548.6 153.4 all-reduce.130
  704.3 75.7 reduce-scatter.5
  959.4 154.2 all-reduce.132
  1117.2 80.5 reduce-scatter.7
  1201.5 156.8 reduce-scatter.11
  1362.8 57.8 all-reduce.134
  1424.8 55.7 reduce-scatter.9
  1484.7 92.3 reduce-scatter.13
where the time goes:
time: 1600 us; the launch traced here: 1590 us
  waiting for transfers between devices  967 us (60%)
  local copies, waits for them, and re-layouts  262 us (16%)
  other arithmetic  146 us (9%)
  matrix products  136 us (8%)
  blocking collectives  54.6 us (3%)
  between operations  16.9 us (1%)
    reduce_scatter x1, waiting for transfers between devices, body(): lax.psum_scatter(matmul_tn(second_low, d_pair_low), 'seq', scatter_dimens...  158 us
    psum x1, waiting for transfers between devices, body(): branch = lax.psum(matmul(mixed_low, proj_out), 'mp')  152 us
    psum x1, waiting for transfers between devices, body(): d_second = lax.psum(d_second_part, 'mp')  141 us
    pad x94, local copies, waits for them, and re-layouts, local_scan(): return lax.associative_scan(link, (carry, fresh), axis=0)  112 us
    psum x1, waiting for transfers between devices, body(): d_first = lax.psum(d_first_part, 'mp')  106 us
    reduce_scatter x1, waiting for transfers between devices, body(): lax.psum_scatter(matmul_tn(hidden_low, cot_low), 'seq', scatter_dimension...  96.5 us
    all_gather x1, waiting for transfers between devices, body(): rows_full = lax.all_gather(stream, 'mp', axis=1, tiled=True)  83.1 us
    slice x92, local copies, waits for them, and re-layouts, local_scan(): return lax.associative_scan(link, (carry, fresh), axis=0)  81.5 us
  transfers between devices with their start and end apart: 13, of which 11 were waited for; matrix products, arithmetic and copies ran while one was open for 21% of the time, Pallas kernels for 0%

commit v1 on v0

--- a/solution.py
+++ b/solution.py
@@ -118,7 +118,12 @@
     groups = gate_recur.shape[0]
     lag = conv_weight.shape[0] - 1
     column = lax.axis_index("mp") * own_width
-    rows_full = lax.all_gather(stream, "mp", axis=1, tiled=True)
+    ring = [stream]
+    for hop in range(3):
+        ring.append(lax.ppermute(ring[-1], "mp", [(dev, (dev + 1) % 4) for dev in range(4)]))
+    rows_full = jnp.roll(
+        jnp.concatenate(ring[::-1], axis=1), (lax.axis_index("mp") + 1) * ring[0].shape[1], axis=1
+    )
     first_norm, first_back = jax.vjp(norm_rows, rows_full, gain_first)
     first_low = first_norm.astype(jnp.bfloat16)
     inner = matmul(first_low, proj_inner)

time: 1600 us -> 1600 us (level)
    all_gather x1 -> x0, waiting for transfers between devices: 83.1 us -> none  [body(): rows_full = lax.all_gather(stream, 'mp', axis=1, tiled=True)]
    ppermute x0 -> x3, waiting for transfers between devices: none -> 75.2 us  [body(): lax.ppermute(ring[-1], 'mp', [(dev, (dev + 1) % 4) for dev in range(4)])]
  transfers between devices with their start and end apart: 13 -> 15, of which waited for: 11 -> 13; matrix products, arithmetic and copies ran while one was open for 21% -> 21% of each run, Pallas kernels for 0% -> 0%
where the time goes in v1:
time: 1600 us; the launch traced here: 1590 us
  waiting for transfers between devices  958 us (60%)
  local copies, waits for them, and re-layouts  272 us (17%)
  other arithmetic  143 us (9%)
  matrix products  136 us (8%)
  blocking collectives  54.6 us (3%)
  between operations  17.2 us (1%)
    reduce_scatter x1, waiting for transfers between devices, body(): lax.psum_scatter(matmul_tn(second_low, d_pair_low), 'seq', scatter_dimens...  158 us
    psum x1, waiting for transfers between devices, body(): branch = lax.psum(matmul(mixed_low, proj_out), 'mp')  152 us
    psum x1, waiting for transfers between devices, body(): d_second = lax.psum(d_second_part, 'mp')  141 us
    pad x94, local copies, waits for them, and re-layouts, local_scan(): return lax.associative_scan(link, (carry, fresh), axis=0)  112 us
    psum x1, waiting for transfers between devices, body(): d_first = lax.psum(d_first_part, 'mp')  106 us
    reduce_scatter x1, waiting for transfers between devices, body(): lax.psum_scatter(matmul_tn(hidden_low, cot_low), 'seq', scatter_dimension...  96.4 us
    slice x92, local copies, waits for them, and re-layouts, local_scan(): return lax.associative_scan(link, (carry, fresh), axis=0)  81.5 us
    ppermute x3, waiting for transfers between devices, body(): lax.ppermute(ring[-1], 'mp', [(dev, (dev + 1) % 4) for dev in range(4)])  75.2 us
  transfers between devices with their start and end apart: 15, of which 13 were waited for; matrix products, arithmetic and copies ran while one was open for 21% of the time, Pallas kernels for 0%

profile of v1, /device:TPU:0, one launch (start us, length us, event | category | flops | bytes accessed | tf_op | source)
XLA Modules:
  0.0 1586.9 jit_solution(229777817571805726)
XLA Ops:
  10.3 25.4 %collective-permute-done = f32[512,512]{1,0:T(8,128)S(1)} collective-permute-done((f32[512,512]{1,0:T(8,128)}, f32[512,512]{1,0:T(8,128)S(1)}, u32[]{:S(2)}, u32[]{:S(2)}) %collective-permute-start) | collective-permute-done | bytes 1048608 | tf_op jit(solution)/shard_map/ppermute | solution.py:123
  36.7 26.2 %collective-permute-done.1 = f32[512,512]{1,0:T(8,128)} collective-permute-done((f32[512,512]{1,0:T(8,128)S(1)}, f32[512,512]{1,0:T(8,128)}, u32[]{:S(2)}, u32[]{:S(2)}) %collective-permute-start.1) | collective-permute-done | bytes 1048608 | tf_op jit(solution)/shard_map/ppermute | solution.py:123
  65.0 23.5 %collective-permute-done.2 = f32[512,512]{1,0:T(8,128)} collective-permute-done((f32[512,512]{1,0:T(8,128)}, f32[512,512]{1,0:T(8,128)}, u32[]{:S(2)}, u32[]{:S(2)}) %collective-permute-start.2) | collective-permute-done | bytes 1048608 | tf_op jit(solution)/shard_map/ppermute | solution.py:123
  241.1 12.3 all-gather.2
  261.6 8.2 all-gather.1
  276.2 7.2 multiply_convert_fusion.4
  288.8 151.6 %all-reduce.129.cloned.1.call-done = f32[512,2048]{1,0:T(8,128)} async-done(((f32[512,2048]{1,0:T(8,128)}), f32[512,2048]{1,0:T(8,128)}) %all-reduce.129.cloned.1.call-update) | async-done | bytes 4194320 | tf_op jit(solution)/shard_map/psum | solution.py:158
  446.5 10.0 fusion.115
  461.6 60.2 %all-gather.6.cloned.1.call-done = f32[512,2048]{1,0:T(8,128)} async-done(((f32[512,512]{1,0:T(8,128)}), f32[512,2048]{1,0:T(8,128)}) %all-gather.6.cloned.1.call-update) | async-done | bytes 4194320 | tf_op jit(solution)/shard_map/all_gather | solution.py:168
  521.8 12.5 multiply_convert_fusion.2
  534.4 6.7 fusion.117
  541.1 8.0 convolution_add_fusion.1
  551.8 9.6 fusion.116
  561.5 141.2 %all-reduce.131.cloned.1.call-done = f32[512,2048]{1,0:T(8,128)} async-done(((f32[512,2048]{1,0:T(8,128)}), f32[512,2048]{1,0:T(8,128)}) %all-reduce.131.cloned.1.call-update) | async-done | bytes 4194320 | tf_op jit(solution)/shard_map/psum | solution.py:176
  712.9 7.2 multiply_reduce_fusion.11
  720.1 9.0 all-gather.3
  732.7 5.7 while.35
  900.1 5.8 multiply_reduce_fusion.6
  922.4 6.1 multiply_reduce_fusion.9
  952.4 6.9 convolution_add_fusion
  959.3 8.6 fusion.25
  967.9 14.3 fusion.8
  988.0 6.1 fusion.30
  994.2 10.6 fusion.34
  1007.6 106.1 %all-reduce.133.cloned.1.call-done = f32[512,2048]{1,0:T(8,128)} async-done(((f32[512,2048]{1,0:T(8,128)}), f32[512,2048]{1,0:T(8,128)}) %all-reduce.133.cloned.1.call-update) | async-done | bytes 4194320 | tf_op jit(solution)/shard_map/psum | solution.py:211
  1113.8 6.6 multiply_reduce_fusion.1
  1120.4 25.1 %all-reduce.122 = (f32[2048]{0:T(1024)}, f32[4,640]{1,0:T(4,128)}, f32[640]{0:T(1024)}, f32[640]{0:T(1024)}, f32[640]{0:T(1024)}, /*index=5*/f32[640]{0:T(1024)}, f32[2048]{0:T(1024)}) all-reduce(f32[2048]{0:T(1024)S(1)} %get-tuple-element.317, f32[4,640]{1,0:T(4,128)S(1)} %pad_maximum_fusion.15, ...), channel_id=1, replica_groups=mesh['seq'=8,'mp'=4] {'seq'}, use_global_device_ids=true, to_apply=%region_15.16 | all-reduce | flops 9216 | bytes 73728 | tf_op jit(solution)/shard_map/psum | solution.py:214
  1148.6 49.1 %reduce-scatter.8.cloned.1.call-done = f32[256,1280]{1,0:T(8,128)} async-done(((f32[2048,1280]{1,0:T(8,128)}), f32[256,1280]{1,0:T(8,128)}) %reduce-scatter.8.cloned.1.call-update) | async-done | bytes 1310736 | tf_op jit(solution)/shard_map/reduce_scatter | solution.py:229
  1200.2 158.1 %reduce-scatter.12.cloned.1.call-done = f32[256,3072]{1,0:T(8,128)} async-done(((f32[2048,3072]{1,0:T(8,128)}), f32[256,3072]{1,0:T(8,128)}) %reduce-scatter.12.cloned.1.call-update) | async-done | bytes 3145744 | tf_op jit(solution)/shard_map/reduce_scatter | solution.py:233
  1362.0 58.6 %all-reduce.135.cloned.1.call-done = (f32[4,160,160]{2,1,0:T(8,128)}, f32[4,160,160]{2,1,0:T(8,128)}) async-done(((f32[4,160,160]{2,1,0:T(8,128)}, f32[4,160,160]{2,1,0:T(8,128)}), (f32[4,160,160]{2,1,0:T(8,128)}, f32[4,160,160]{2,1,0:T(8,128)})) %all-reduce.135.cloned.1.call-update) | async-done | bytes 819216 | tf_op jit(solution)/shard_map/psum | solution.py:214
  1420.6 60.1 %reduce-scatter.10.cloned.1.call-done = f32[80,2048]{1,0:T(8,128)} async-done(((f32[640,2048]{1,0:T(8,128)}), f32[80,2048]{1,0:T(8,128)}) %reduce-scatter.10.cloned.1.call-update) | async-done | bytes 655376 | tf_op jit(solution)/shard_map/reduce_scatter | solution.py:232
  1480.7 96.4 %reduce-scatter.14.cloned.1.call-done = f32[192,2048]{1,0:T(8,128)} async-done(((f32[1536,2048]{1,0:T(8,128)}), f32[192,2048]{1,0:T(8,128)}) %reduce-scatter.14.cloned.1.call-update) | async-done | bytes 1572880 | tf_op jit(solution)/shard_map/reduce_scatter | solution.py:234
  (827 shorter events, 437.6 us)
Async XLA Ops:
  7.2 269.0 %copy-start = (bf16[2048,640]{1,0:T(8,128)(2,1)S(1)}, bf16[2048,640]{1,0:T(8,128)(2,1)}, u32[]{:S(2)}) copy-start(bf16[2048,640]{1,0:T(8,128)(2,1)} %param.38) | copy-start | bytes 7864324
  7.2 433.2 %all-reduce.129.cloned.1.call-start = ((), (), s32[]{:S(2)}) async-start(), calls=%async_computation.5 | async-start | bytes 8388608 | tf_op jit(solution)/shard_map/psum | solution.py:158
  7.2 28.5 %collective-permute-start = (f32[512,512]{1,0:T(8,128)}, f32[512,512]{1,0:T(8,128)S(1)}, u32[]{:S(2)}, u32[]{:S(2)}) collective-permute-start(f32[512,512]{1,0:T(8,128)} %param.34), channel_id=1, source_target_pairs={{0,1},{1,2},{2,3},{3,0},{4,5},{5,6},{6,7},{7,4},{8,9},{9,10},{10,1... | collective-permute-start | bytes 3145736 | tf_op jit(solution)/shard_map/ppermute | solution.py:123
  36.7 26.2 %collective-permute-start.1 = (f32[512,512]{1,0:T(8,128)S(1)}, f32[512,512]{1,0:T(8,128)}, u32[]{:S(2)}, u32[]{:S(2)}) collective-permute-start(f32[512,512]{1,0:T(8,128)S(1)} %collective-permute-done), channel_id=1, source_target_pairs={{0,1},{1,2},{2,3},{3,0},{4,5},{5,6},{6,7},{7,4},{8,9},{9,10},{10,1... | collective-permute-start | bytes 3145736 | tf_op jit(solution)/shard_map/ppermute | solution.py:123
  62.9 25.5 %collective-permute-start.2 = (f32[512,512]{1,0:T(8,128)}, f32[512,512]{1,0:T(8,128)}, u32[]{:S(2)}, u32[]{:S(2)}) collective-permute-start(f32[512,512]{1,0:T(8,128)} %collective-permute-done.1), channel_id=1, source_target_pairs={{0,1},{1,2},{2,3},{3,0},{4,5},{5,6},{6,7},{7,4},{8,9},{9,10},{10,1... | collective-permute-start | bytes 3145736 | tf_op jit(solution)/shard_map/ppermute | solution.py:123
  63.6 58.5 %copy-start.118 = (f32[512]{0:T(512)}, f32[512]{0:T(512)S(1)}, u32[]{:S(2)}) copy-start(f32[512]{0:T(512)S(1)} %broadcast_subtract_fusion) | copy-start | bytes 6148
  64.2 37.6 %copy-start.183 = (f32[3,1]{0,1:T(1,128)}, f32[3,1]{0,1:T(1,128)S(1)}, u32[]{:S(2)}) copy-start(f32[3,1]{0,1:T(1,128)S(1)} %rev.14) | copy-start | bytes 40
  64.2 40.8 %copy-start.163 = (f32[512,1]{0,1:T(1,128)}, f32[512,1]{0,1:T(1,128)S(1)}, u32[]{:S(2)}) copy-start(f32[512,1]{0,1:T(1,128)S(1)} %get-tuple-element.399) | copy-start | bytes 6148
  64.2 40.8 %copy-start.165 = (f32[512,1]{0,1:T(1,128)}, f32[512,1]{0,1:T(1,128)S(1)}, u32[]{:S(2)}) copy-start(f32[512,1]{0,1:T(1,128)S(1)} %get-tuple-element.400) | copy-start | bytes 6148
  64.9 57.2 %copy-start.120 = (f32[640]{0:T(1024)}, f32[640]{0:T(1024)S(1)}, u32[]{:S(2)}) copy-start(f32[640]{0:T(1024)S(1)} %broadcast_multiply_fusion.3) | copy-start | bytes 7684
  102.9 2.1 collective-permute-start.3
  104.8 17.4 %copy-start.169 = (f32[512]{0:T(512)}, f32[512]{0:T(512)S(1)}, u32[]{:S(2)}) copy-start(f32[512]{0:T(512)S(1)} %convert_element_type.44) | copy-start | bytes 6148
  131.1 22.3 %copy-start.17 = (f32[256,640]{1,0:T(8,128)}, f32[256,640]{1,0:T(8,128)S(1)}, u32[]{:S(2)}) copy-start(f32[256,640]{1,0:T(8,128)S(1)} %slice.594) | copy-start | bytes 1966084
  288.0 233.9 %all-gather.6.cloned.1.call-start = ((), (), s32[]{:S(2)}) async-start(), calls=%async_computation.7 | async-start | bytes 5242880 | tf_op jit(solution)/shard_map/all_gather | solution.py:168
  288.7 155.7 %copy-start.132 = (f32[2048]{0:T(1024)S(1)}, f32[2048]{0:T(1024)}, u32[]{:S(2)}) copy-start(f32[2048]{0:T(1024)} %param.47) | copy-start | bytes 24580
  288.7 414.0 %all-reduce.131.cloned.1.call-start = ((), (), s32[]{:S(2)}) async-start(), calls=%async_computation.8 | async-start | bytes 8388608 | tf_op jit(solution)/shard_map/psum | solution.py:176
  549.1 455.8 %reduce-scatter.6.cloned.1.call-start = ((), (), s32[]{:S(2)}) async-start(), calls=%async_computation.6 | async-start | bytes 5242880 | tf_op jit(solution)/shard_map/reduce_scatter | solution.py:166
  561.5 141.3 %copy-start.173 = (f32[512]{0:T(512)S(1)}, f32[512]{0:T(512)}, u32[]{:S(2)}) copy-start(f32[512]{0:T(512)} %copy-done.172) | copy-start | bytes 6148
  561.5 552.3 %all-reduce.133.cloned.1.call-start = ((), (), s32[]{:S(2)}) async-start(), calls=%async_computation.9 | async-start | bytes 8388608 | tf_op jit(solution)/shard_map/psum | solution.py:211
  803.9 14.5 copy-start.39
  831.6 12.4 slice-start.7
  946.3 5.4 collective-permute-start.4
  959.3 238.5 %reduce-scatter.8.cloned.1.call-start = ((), (), s32[]{:S(2)}) async-start(), calls=%async_computation.10 | async-start | bytes 11796480 | tf_op jit(solution)/shard_map/reduce_scatter | solution.py:229
  967.9 390.4 %reduce-scatter.12.cloned.1.call-start = ((), (), s32[]{:S(2)}) async-start(), calls=%async_computation.12 | async-start | bytes 28311552 | tf_op jit(solution)/shard_map/reduce_scatter | solution.py:233
  982.3 438.3 %all-reduce.135.cloned.1.call-start = ((), (), s32[]{:S(2)}) async-start(), calls=%async_computation.14 | async-start | bytes 2621440 | tf_op jit(solution)/shard_map/psum | solution.py:214
  986.9 493.8 %reduce-scatter.10.cloned.1.call-start = ((), (), s32[]{:S(2)}) async-start(), calls=%async_computation.11 | async-start | bytes 5898240 | tf_op jit(solution)/shard_map/reduce_scatter | solution.py:232
  994.1 582.9 %reduce-scatter.14.cloned.1.call-start = ((), (), s32[]{:S(2)}) async-start(), calls=%async_computation.13 | async-start | bytes 14155776 | tf_op jit(solution)/shard_map/reduce_scatter | solution.py:234
  1004.8 108.9 %copy-start.162 = (f32[2048]{0:T(1024)S(1)}, f32[2048]{0:T(1024)}, u32[]{:S(2)}) copy-start(f32[2048]{0:T(1024)} %param.36) | copy-start | bytes 24580
  1004.9 108.9 %copy-start.168 = (f32[512]{0:T(512)S(1)}, f32[512]{0:T(512)}, u32[]{:S(2)}) copy-start(f32[512]{0:T(512)} %copy-done.167) | copy-start | bytes 6148
  1007.6 112.8 %copy-start.171 = (f32[2048]{0:T(1024)S(1)}, f32[2048]{0:T(1024)}, u32[]{:S(2)}) copy-start(f32[2048]{0:T(1024)} %get-tuple-element.315) | copy-start | bytes 24580
  1007.6 137.9 %copy-start.176 = (f32[512]{0:T(512)S(1)}, f32[512]{0:T(512)}, u32[]{:S(2)}) copy-start(f32[512]{0:T(512)} %copy-done.175) | copy-start | bytes 6148
  1420.6 158.5 %copy-start.75 = (f32[4,160,160]{2,1,0:T(8,128)S(1)}, f32[4,160,160]{2,1,0:T(8,128)}, u32[]{:S(2)}) copy-start(f32[4,160,160]{2,1,0:T(8,128)} %get-tuple-element.666) | copy-start | bytes 1228804
  (188 other events, 855.6 us)
Sparse Core Ops, SparseCore 0:
  288.1 152.2 all-reduce.128
  442.0 79.7 all-gather.5
  549.2 153.4 all-reduce.130
  704.9 75.7 reduce-scatter.5
  959.4 154.3 all-reduce.132
  1117.1 80.5 reduce-scatter.7
  1201.4 156.8 reduce-scatter.11
  1362.6 57.8 all-reduce.134
  1424.9 55.7 reduce-scatter.9
  1484.6 92.3 reduce-scatter.13
